TPU v7x, 32 devices: a whole 2x2x4 slice. The times are simulated.
32 devices in a mesh: rows: 8 (over y, x, core), tp: 4 (over z).
Axes of the slice: x: 2, y: 2, z: 4, core: 2. Of those that a mesh axis runs over, the one named last changes fastest.
Arguments:
- first_query: float32 [9216, 9216], P('rows', 'tp'), may hold values from -0.09375 to 0.09375
- second_query: float32 [9216, 9216], P('rows', 'tp'), may hold values from -0.0625 to 0.0625
- first_key: float32 [9216, 9216], P('rows', 'tp'), may hold values from -0.09375 to 0.09375
- second_key: float32 [9216, 9216], P('rows', 'tp'), may hold values from -0.0625 to 0.0625
- first_value: float32 [9216, 9216], P('rows', 'tp'), may hold values from -0.09375 to 0.09375
- second_value: float32 [9216, 9216], P('rows', 'tp'), may hold values from -0.0625 to 0.0625
- mix_share: float32 [9216], P('rows'), may hold values from 0.2 to 0.8
- norm_train: float32 [9216], P(('rows', 'tp')), may hold values from 0.25 to 1.75
- norm_step: float32 [9216], P(('rows', 'tp')), may hold values from -0.3 to 0.3
Outputs:
- serving_query: bfloat16 [9216, 9216], P(None, ('tp', 'rows'))
- serving_key: bfloat16 [9216, 9216], P(None, ('tp', 'rows'))
- serving_value: bfloat16 [9216, 9216], P(None, ('tp', 'rows'))
- scale_query: float32 [9216], P(('tp', 'rows'))
- scale_key: float32 [9216], P(('tp', 'rows'))
- scale_value: float32 [9216], P(('tp', 'rows'))
- serve_norm: bfloat16 [9216], replicated
All inputs are finite; a program needn't handle non-finite values.
Results may differ from a plain program's by a relative error of at most 0.001.
Values may be sent and summed in bfloat16 or wider, within the bound.
A program may use at most 192 MiB of HBM per device.

v0:
```python
import jax
import jax.numpy as jnp
from jax import lax
from jax.sharding import PartitionSpec as P


def per_device(
    first_query,
    second_query,
    first_key,
    second_key,
    first_value,
    second_value,
    mix_share,
    norm_train,
    norm_step,
):
    whole_query = mix_share[:, None] * first_query + (1.0 - mix_share[:, None]) * second_query
    whole_key = mix_share[:, None] * first_key + (1.0 - mix_share[:, None]) * second_key
    whole_value = mix_share[:, None] * first_value + (1.0 - mix_share[:, None]) * second_value
    scale_query, scale_key, scale_value = lax.pmax(
        (
            jnp.max(jnp.abs(whole_query), axis=0),
            jnp.max(jnp.abs(whole_key), axis=0),
            jnp.max(jnp.abs(whole_value), axis=0),
        ),
        "rows",
    )
    narrow_query, narrow_key, narrow_value = (
        (whole_query / scale_query).astype(jnp.bfloat16),
        (whole_key / scale_key).astype(jnp.bfloat16),
        (whole_value / scale_value).astype(jnp.bfloat16),
    )
    serving_query, serving_key, serving_value = (
        lax.all_to_all(narrow_query, "rows", split_axis=1, concat_axis=0, tiled=True),
        lax.all_to_all(narrow_key, "rows", split_axis=1, concat_axis=0, tiled=True),
        lax.all_to_all(narrow_value, "rows", split_axis=1, concat_axis=0, tiled=True),
    )
    place = lax.axis_index("rows")
    scale_query = lax.dynamic_slice_in_dim(
        scale_query, place * serving_query.shape[1], serving_query.shape[1]
    )
    scale_key = lax.dynamic_slice_in_dim(
        scale_key, place * serving_key.shape[1], serving_key.shape[1]
    )
    scale_value = lax.dynamic_slice_in_dim(
        scale_value, place * serving_value.shape[1], serving_value.shape[1]
    )
    serve_norm = lax.all_gather(
        (norm_train + norm_step).astype(jnp.bfloat16), ("rows", "tp"), axis=0, tiled=True
    )
    return (
        serving_query,
        serving_key,
        serving_value,
        scale_query,
        scale_key,
        scale_value,
        serve_norm,
    )


def solution(mesh):
    return jax.shard_map(
        per_device,
        mesh=mesh,
        in_specs=(
            P("rows", "tp"),
            P("rows", "tp"),
            P("rows", "tp"),
            P("rows", "tp"),
            P("rows", "tp"),
            P("rows", "tp"),
            P("rows"),
            P(("rows", "tp")),
            P(("rows", "tp")),
        ),
        out_specs=(
            P(None, ("tp", "rows")),
            P(None, ("tp", "rows")),
            P(None, ("tp", "rows")),
            P(("tp", "rows")),
            P(("tp", "rows")),
            P(("tp", "rows")),
            P(),
        ),
        check_vma=False,
    )
```

profile of v0, /device:TPU:0, one launch (start us, length us, event | category | flops | bytes accessed | tf_op | source)
XLA Modules:
  0.0 396.2 jit_solution(8847732719092262777)
XLA Ops:
  0.6 12.7 %copy.25 = f32[1152,2304]{0,1:T(8,128)} copy(f32[1152,2304]{1,0:T(8,128)} %param.9) | data formatting | bytes 21233664 | tf_op args[0]
  13.3 12.7 %copy.26 = f32[1152,2304]{0,1:T(8,128)} copy(f32[1152,2304]{1,0:T(8,128)} %param.10) | data formatting | bytes 21233664 | tf_op args[1]
  26.0 12.7 %copy.28 = f32[1152,2304]{0,1:T(8,128)} copy(f32[1152,2304]{1,0:T(8,128)} %param.11) | data formatting | bytes 21233664 | tf_op args[2]
  38.7 12.7 %copy.29 = f32[1152,2304]{0,1:T(8,128)} copy(f32[1152,2304]{1,0:T(8,128)} %param.12) | data formatting | bytes 21233664 | tf_op args[3]
  51.4 12.7 %copy.31 = f32[1152,2304]{0,1:T(8,128)} copy(f32[1152,2304]{1,0:T(8,128)} %param.13) | data formatting | bytes 21233664 | tf_op args[4]
  64.1 12.7 %copy.32 = f32[1152,2304]{0,1:T(8,128)} copy(f32[1152,2304]{1,0:T(8,128)} %param.14) | data formatting | bytes 21233664 | tf_op args[5]
  76.7 21.5 %abs_reduce_fusion = (f32[2304]{0:T(1024)S(1)}, f32[2304]{0:T(1024)S(1)}, f32[2304]{0:T(1024)S(1)}) fusion(f32[1152,2304]{0,1:T(8,128)} %copy.32, f32[1152]{0:T(1024)S(1)} %broadcast_subtract_fusion, f32[1152,2304]{0,1:T(8,128)} %copy.31, f32[1152]{0:T(1024)S(1)} %copy-done, f32[1152,2304]{0,1:T(8,128)} %copy.29, f32[1152,2304]{0,1:T(8,128)} %copy.28, ...), kind=kLoop, calls=%fused_computation.1 | loop fusion | flops 39806208 | bytes 63737856 | tf_op jit(solution)/shard_map/reduce_max | solution.py:25
  98.3 25.9 %all-reduce.1 = (f32[2304]{0:T(1024)S(1)}, f32[2304]{0:T(1024)S(1)}, f32[2304]{0:T(1024)S(1)}) all-reduce(f32[2304]{0:T(1024)S(1)} %get-tuple-element.9, f32[2304]{0:T(1024)S(1)} %get-tuple-element.8, f32[2304]{0:T(1024)S(1)} %get-tuple-element.7), channel_id=1, replica_groups=mesh['rows'=8,'tp'=4] {'rows'}, use_global_device_ids=true, to_apply=%region_1.0 | all-reduce | flops 6912 | bytes 55296 | tf_op jit(solution)/shard_map/pmax | solution.py:21
  124.1 27.4 %divide_convert_fusion = (bf16[1152,2304]{0,1:T(8,128)(2,1)}, bf16[1152,2304]{0,1:T(8,128)(2,1)}, bf16[1152,2304]{0,1:T(8,128)(2,1)}) fusion(f32[2304]{0:T(1024)S(1)} %get-tuple-element.12, f32[1152,2304]{0,1:T(8,128)} %copy.32, f32[1152]{0:T(1024)S(1)} %broadcast_subtract_fusion, f32[1152,2304]{0,1:T(8,128)} %copy.31, f32[1152]{0:T(1024)S(1)} %copy-done, ...), kind=kLoop, calls=%fused_computation | loop fusion | flops 39813120 | bytes 79663104 | tf_op jit(solution)/shard_map/convert_element_type | solution.py:32
  151.6 65.9 %all_to_all.57 = bf16[1152,8,288]{0,2,1:T(8,128)(2,1)} all-to-all(bf16[1152,8,288]{0,2,1:T(8,128)(2,1)} %bitcast.20), channel_id=1, replica_groups=mesh['rows'=8,'tp'=4] {'rows'}, dimensions={1} | all-to-all | bytes 10616832 | tf_op jit(solution)/shard_map/all_to_all | solution.py:37
  217.5 0.0 copy-start.2
  217.5 64.5 %all_to_all.58 = bf16[1152,8,288]{0,2,1:T(8,128)(2,1)} all-to-all(bf16[1152,8,288]{0,2,1:T(8,128)(2,1)S(1)} %bitcast.19), channel_id=1, replica_groups=mesh['rows'=8,'tp'=4] {'rows'}, dimensions={1} | all-to-all | bytes 10616832 | tf_op jit(solution)/shard_map/all_to_all | solution.py:35
  282.0 4.7 %all-to-all-start.1 = ((bf16[1152,8,288]{0,2,1:T(8,128)(2,1)}), bf16[1152,8,288]{0,2,1:T(8,128)(2,1)}, u32[]{:S(2)}, u32[]{:S(2)}) async-start(bf16[1152,8,288]{0,2,1:T(8,128)(2,1)} %bitcast.16), calls=%async_computation.1 | async-start | bytes 10616832 | tf_op jit(solution)/shard_map/all_to_all | solution.py:36
  286.7 0.0 slice-start
  286.7 0.7 dynamic_slice.10
  287.4 0.7 dynamic_slice.11
  288.0 0.7 dynamic_slice.9
  288.7 0.0 copy-done.2
  288.7 0.3 dynamic-update-slice
  288.9 92.5 %all-reduce = bf16[9216]{0:T(1024)(128)(2,1)} all-reduce(bf16[9216]{0:T(1024)(128)(2,1)S(1)} %dynamic-update-slice), channel_id=1, replica_groups=mesh['rows'=8,'tp'=4] {'rows','tp'}, use_global_device_ids=true, to_apply=%add | all-reduce | flops 9216 | bytes 36864
  381.5 5.9 %copy.36 = bf16[8,36,8,1152]{3,2,0,1:T(8,128)(2,1)} copy(bf16[8,36,8,1152]{3,2,1,0:T(8,128)(2,1)} %bitcast.12) | data formatting | bytes 10616832 | tf_op jit(solution)/shard_map/all_to_all | solution.py:37
  387.3 3.2 copy.34
  390.5 0.0 all-to-all-done.1
  390.5 5.7 %copy.35 = bf16[8,36,8,1152]{3,2,0,1:T(8,128)(2,1)} copy(bf16[8,36,8,1152]{3,2,1,0:T(8,128)(2,1)} %bitcast.8) | data formatting | bytes 10616832 | tf_op jit(solution)/shard_map/all_to_all | solution.py:36
  (16 shorter events, 0.0 us)
Async XLA Ops:
  64.1 12.7 %copy-start = (f32[1152]{0:T(1024)S(1)}, f32[1152]{0:T(1024)}, u32[]{:S(2)}) copy-start(f32[1152]{0:T(1024)} %param.15) | copy-start | bytes 13828
  151.6 66.0 %slice-start.2 = ((s8[5308416]{0:T(1024)(128)(4,1)}), s8[4194304]{0:T(1024)(128)(4,1)S(1)}, s32[]{:S(2)}) async-start(s8[5308416]{0:T(1024)(128)(4,1)} %bitcast.17), calls=%async_computation.5 | async-start | bytes 8388608
  151.6 66.0 %slice-start.3 = ((s8[5308416]{0:T(1024)(128)(4,1)}), s8[1114112]{0:T(1024)(128)(4,1)S(1)}, s32[]{:S(2)}) async-start(s8[5308416]{0:T(1024)(128)(4,1)} %bitcast.17), calls=%async_computation.6 | async-start | bytes 2228224
  217.5 71.1 %copy-start.1 = (f32[288]{0:T(512)S(1)}, f32[288]{0:T(512)}, u32[]{:S(2)}) copy-start(f32[288]{0:T(512)} %param.16) | copy-start | bytes 3460
  217.5 71.1 %copy-start.2 = (f32[288]{0:T(512)S(1)}, f32[288]{0:T(512)}, u32[]{:S(2)}) copy-start(f32[288]{0:T(512)} %param.17) | copy-start | bytes 3460
  282.0 108.5 %all-to-all-start.1 = ((bf16[1152,8,288]{0,2,1:T(8,128)(2,1)}), bf16[1152,8,288]{0,2,1:T(8,128)(2,1)}, u32[]{:S(2)}, u32[]{:S(2)}) async-start(bf16[1152,8,288]{0,2,1:T(8,128)(2,1)} %bitcast.16), calls=%async_computation.1 | async-start | bytes 10616832 | tf_op jit(solution)/shard_map/all_to_all | solution.py:36
  286.7 100.6 %slice-start = ((s8[5308416]{0:T(1024)(128)(4,1)}), s8[1114112]{0:T(1024)(128)(4,1)S(1)}, s32[]{:S(2)}) async-start(s8[5308416]{0:T(1024)(128)(4,1)} %bitcast.13), calls=%async_computation.3 | async-start | bytes 2228224
  381.5 5.9 %slice-start.1 = ((s8[5308416]{0:T(1024)(128)(4,1)}), s8[4194304]{0:T(1024)(128)(4,1)S(1)}, s32[]{:S(2)}) async-start(s8[5308416]{0:T(1024)(128)(4,1)} %bitcast.13), calls=%async_computation.4 | async-start | bytes 8388608
where the time goes:
time: 398 us; the launch traced here: 396 us
  blocking collectives  249 us (63%)
  local copies, waits for them, and re-layouts  93.1 us (23%)
  other arithmetic  49 us (12%)
  starting transfers between devices  4.65 us (1%)
    unnamed x1, blocking collectives  92.5 us
    unnamed x22, local copies, waits for them, and re-layouts  76.4 us
    all_to_all x1, blocking collectives, per_device(): lax.all_to_all(narrow_value, 'rows', split_axis=1, concat_axis=0, tiled=T...  65.9 us
    all_to_all x1, blocking collectives, per_device(): lax.all_to_all(narrow_query, 'rows', split_axis=1, concat_axis=0, tiled=T...  64.5 us
    convert_element_type x1, other arithmetic, per_device(): (whole_value / scale_value).astype(jnp.bfloat16)  27.4 us
    pmax x1, blocking collectives, per_device(): lax.pmax((jnp.max(jnp.abs(whole_query), axis=0), jnp.max(jnp.abs(whole_ke...  25.9 us
    reduce_max x1, other arithmetic, per_device(): jnp.max(jnp.abs(whole_value), axis=0)  21.5 us
  transfers between devices with their start and end apart: 1, of which 0 were waited for; matrix products, arithmetic and copies ran while one was open for 3% of the time, Pallas kernels for 0%

commit v1 on v0

--- a/solution.py
+++ b/solution.py
@@ -1,10 +1,166 @@
+import functools
+import math
+
 import jax
 import jax.numpy as jnp
 from jax import lax
+from jax.experimental import pallas as pl
+from jax.experimental.pallas import tpu as pltpu
 from jax.sharding import PartitionSpec as P
 
-
-def per_device(
+MESH = pl.DeviceIdType.MESH
+LANES = 128
+
+
+def kernel(
+    n, tp, group, share, deep,
+    mix_ref, norm_ref, fq, sq, fk, sk, fv, sv,
+    out_q, out_k, out_v, scale_ref, norm_out,
+    first, second, whole, narrow, peaks,
+    load_sem, peak_send, peak_recv, send_sem, recv_sem, own_sem, norm_send, norm_recv,
+):
+    row, col = lax.axis_index("rows"), lax.axis_index("tp")
+    wide = group * share
+    per = n // group
+    units = 3 * per
+    pairs = ((fq, sq), (fk, sk), (fv, sv))
+    outs = (out_q, out_k, out_v)
+    count = n * tp
+    me = row * tp + col
+
+    def loads(u):
+        slot = u % 2
+        columns = pl.ds((u % per) * wide, wide)
+        a, b = pairs[u // per]
+        return (
+            pltpu.make_async_copy(a.at[:, columns], first.at[slot], load_sem.at[slot, 0]),
+            pltpu.make_async_copy(b.at[:, columns], second.at[slot], load_sem.at[slot, 1]),
+        )
+
+    def norm_copy(k, target, origin):
+        return pltpu.make_async_remote_copy(
+            src_ref=norm_ref.at[0],
+            dst_ref=norm_out.at[origin],
+            send_sem=norm_send.at[k],
+            recv_sem=norm_recv.at[k],
+            device_id=(target // tp, target % tp),
+            device_id_type=MESH,
+        )
+
+    def peak_copy(u, k, target, origin):
+        return pltpu.make_async_remote_copy(
+            src_ref=peaks.at[u, origin],
+            dst_ref=peaks.at[u, origin],
+            send_sem=peak_send.at[u, k],
+            recv_sem=peak_recv.at[u, k],
+            device_id=(target, col),
+            device_id_type=MESH,
+        )
+
+    def share_copy(m, k, target, origin, u, j):
+        return pltpu.make_async_remote_copy(
+            src_ref=narrow.at[u, pl.ds(pl.multiple_of(j * share, share), share), :],
+            dst_ref=outs[m].at[:, pl.ds(pl.multiple_of(origin * deep, LANES), deep)],
+            send_sem=send_sem.at[m, k],
+            recv_sem=recv_sem.at[m, k],
+            device_id=(target, col),
+            device_id_type=MESH,
+        )
+
+    def own_copy(u, j):
+        m = u // per
+        return pltpu.make_async_copy(
+            narrow.at[u, pl.ds(pl.multiple_of(j * share, share), share), :],
+            outs[m].at[:, pl.ds(pl.multiple_of(row * deep, LANES), deep)],
+            own_sem.at[m],
+        )
+
+    def mix(u):
+        slot = u % 2
+
+        def step(i, top):
+            rows = pl.ds(pl.multiple_of(i * 16, 16), 16)
+            part = jnp.concatenate([mix_ref[rows, :]] * (wide // LANES), axis=1)
+            value = part * first[slot, rows, :] + (1.0 - part) * second[slot, rows, :]
+            whole[slot, rows, :] = value
+            size = jnp.abs(value)
+            return jnp.maximum(top, jnp.maximum(size[:8], size[8:]))
+
+        top = lax.fori_loop(0, deep // 16, step, jnp.zeros((8, wide), jnp.float32))
+        peaks[u, row] = jnp.max(top, axis=0, keepdims=True)
+
+    def narrow_down(u):
+        slot = u % 2
+        scale = jnp.max(peaks[u], axis=0)
+        scale_ref[u] = scale
+        inverse = 1.0 / scale
+
+        def step(i, carry):
+            rows = pl.ds(pl.multiple_of(i * LANES, LANES), LANES)
+            for c in range(wide // LANES):
+                cut = slice(c * LANES, (c + 1) * LANES)
+                value = whole[slot, rows, cut] * inverse[:, cut]
+                narrow[u, cut, rows] = value.T.astype(jnp.bfloat16)
+            return carry
+
+        lax.fori_loop(0, deep // LANES, step, 0)
+
+    def each(lower, upper, body):
+        def step(k, carry):
+            body(k)
+            return carry
+
+        lax.fori_loop(lower, upper, step, 0)
+
+    for u in range(min(2, units)):
+        for copy in loads(u):
+            copy.start()
+    for u in range(units + 1):
+        if u < units:
+            for copy in loads(u):
+                copy.wait()
+            mix(u)
+            if u + 2 < units:
+                for copy in loads(u + 2):
+                    copy.start()
+            each(1, n, lambda k: peak_copy(u, k, (row + k) % n, row).start())
+        if u == 0:
+            each(1, count, lambda k: norm_copy(k, (me + k) % count, me).start())
+            norm_out[me] = norm_ref[0]
+        if u >= 1:
+            v = u - 1
+            each(1, n, lambda k: peak_copy(v, k, row, (row + n - k) % n).wait_recv())
+            narrow_down(v)
+            base = (v % per) * group
+
+            def send(j):
+                place = (row + j) % group
+                target = base + place
+                k = (target + n - row) % n
+
+                @pl.when(target != row)
+                def _():
+                    share_copy(v // per, k, target, row, v, place).start()
+
+                @pl.when(target == row)
+                def _():
+                    own_copy(v, place).start()
+
+            each(0, group, send)
+
+    each(1, count, lambda k: norm_copy(k, me, (me + count - k) % count).wait_recv())
+    each(1, count, lambda k: norm_copy(k, me, me).wait_send())
+    for u in range(units):
+        each(1, n, lambda k: peak_copy(u, k, row, row).wait_send())
+    for m in range(3):
+        pltpu.make_async_copy(
+            narrow.at[0, pl.ds(0, share), :], outs[m].at[:, pl.ds(0, deep)], own_sem.at[m]
+        ).wait()
+        each(1, n, lambda k: share_copy(m, k, row, (row + n - k) % n, m * per, 0).wait_recv())
+        each(1, n, lambda k: share_copy(m, k, row, row, m * per, 0).wait_send())
+
+
+def plain_device(
     first_query,
     second_query,
     first_key,
@@ -60,29 +216,66 @@
     )
 
 
+def per_device(n, tp, fq, sq, fk, sk, fv, sv, mix_share, norm_train, norm_step):
+    deep, columns = fq.shape
+    share = columns // n
+    group = LANES // math.gcd(share, LANES)
+    if deep % LANES or share % 16 or n % group:
+        return plain_device(fq, sq, fk, sk, fv, sv, mix_share, norm_train, norm_step)
+    wide = group * share
+    units = 3 * (n // group)
+    count = n * tp
+    length = norm_train.shape[0]
+    room = -(-length // LANES) * LANES
+    mix = jnp.broadcast_to(mix_share[:, None], (deep, LANES))
+    norm = jnp.pad(norm_train + norm_step, (0, room - length)).reshape(1, 1, room)
+    vmem = pl.BlockSpec(memory_space=pltpu.VMEM)
+    hbm = pl.BlockSpec(memory_space=pl.ANY)
+    out = jax.ShapeDtypeStruct((share, n * deep), jnp.bfloat16)
+    dma = pltpu.SemaphoreType.DMA
+    q, k, v, scales, norms = pl.pallas_call(
+        functools.partial(kernel, n, tp, group, share, deep),
+        name="mix_and_spread",
+        out_shape=(
+            out,
+            out,
+            out,
+            jax.ShapeDtypeStruct((units, 1, wide), jnp.float32),
+            jax.ShapeDtypeStruct((count, 1, room), jnp.float32),
+        ),
+        in_specs=[vmem, vmem] + [hbm] * 6,
+        out_specs=(hbm, hbm, hbm, vmem, vmem),
+        scratch_shapes=[
+            pltpu.VMEM((2, deep, wide), jnp.float32),
+            pltpu.VMEM((2, deep, wide), jnp.float32),
+            pltpu.VMEM((2, deep, wide), jnp.float32),
+            pltpu.VMEM((units, wide, deep), jnp.bfloat16),
+            pltpu.VMEM((units, n, 1, wide), jnp.float32),
+            dma((2, 2)),
+            dma((units, n)),
+            dma((units, n)),
+            dma((3, n)),
+            dma((3, n)),
+            dma((3,)),
+            dma((count,)),
+            dma((count,)),
+        ],
+        compiler_params=pltpu.CompilerParams(
+            has_side_effects=True, vmem_limit_bytes=60 * 1024 * 1024
+        ),
+    )(mix, norm, fq, sq, fk, sk, fv, sv)
+    scales = scales.reshape(3, columns)
+    place = lax.axis_index("rows") * share
+    own = lax.dynamic_slice(scales, (0, place), (3, share))
+    serve_norm = norms[:, 0, :length].reshape(count * length).astype(jnp.bfloat16)
+    return q.T, k.T, v.T, own[0], own[1], own[2], serve_norm
+
+
 def solution(mesh):
     return jax.shard_map(
-        per_device,
+        functools.partial(per_device, mesh.shape["rows"], mesh.shape["tp"]),
         mesh=mesh,
-        in_specs=(
-            P("rows", "tp"),
-            P("rows", "tp"),
-            P("rows", "tp"),
-            P("rows", "tp"),
-            P("rows", "tp"),
-            P("rows", "tp"),
-            P("rows"),
-            P(("rows", "tp")),
-            P(("rows", "tp")),
-        ),
-        out_specs=(
-            P(None, ("tp", "rows")),
-            P(None, ("tp", "rows")),
-            P(None, ("tp", "rows")),
-            P(("tp", "rows")),
-            P(("tp", "rows")),
-            P(("tp", "rows")),
-            P(),
-        ),
+        in_specs=(P("rows", "tp"),) * 6 + (P("rows"), P(("rows", "tp")), P(("rows", "tp"))),
+        out_specs=(P(None, ("tp", "rows")),) * 3 + (P(("tp", "rows")),) * 3 + (P(),),
         check_vma=False,
     )

time: 398 us -> 221 us (0.56)
  blocking collectives: 249 us -> 0 us
  Pallas kernels: 0 us -> 203 us
  local copies, waits for them, and re-layouts: 93.1 us -> 15.8 us
  other arithmetic: 49 us -> 1.51 us
  starting transfers between devices: 4.65 us -> 0 us
    pallas_call x0 -> x1, Pallas kernels: none -> 203 us  [per_device(): pl.pallas_call(functools.partial(kernel, n, tp, group, share, deep), name...]
    all_to_all x2 -> x0, blocking collectives: 130 us -> none  [the longest x1 65.9 us: per_device(): lax.all_to_all(narrow_value, 'rows', split_axis=1, concat_axis=0, tiled=T...]
    unnamed x1 -> x0, blocking collectives: 92.5 us -> none
    unnamed x22 -> x9, local copies, waits for them, and re-layouts: 76.4 us -> 11.2 us
    convert_element_type x2 -> x0, other arithmetic: 27.4 us -> none  [the longest x1 27.4 us: per_device(): (whole_value / scale_value).astype(jnp.bfloat16)]
    pmax x1 -> x0, blocking collectives: 25.9 us -> none  [per_device(): lax.pmax((jnp.max(jnp.abs(whole_query), axis=0), jnp.max(jnp.abs(whole_ke...]
    reduce_max x1 -> x0, other arithmetic: 21.5 us -> none  [per_device(): jnp.max(jnp.abs(whole_value), axis=0)]
    all_to_all x3 -> x0, local copies, waits for them, and re-layouts: 14.7 us -> none  [the longest x1 5.85 us: per_device(): lax.all_to_all(narrow_value, 'rows', split_axis=1, concat_axis=0, tiled=T...]
  transfers between devices with their start and end apart: 1 -> 0, of which waited for: 0 -> 0; matrix products, arithmetic and copies ran while one was open for 3% -> 0% of each run, Pallas kernels for 0% -> 0%
where the time goes in v1:
time: 221 us
  Pallas kernels  203 us (92%)
  local copies, waits for them, and re-layouts  15.8 us (7%)
    pallas_call x1, Pallas kernels, per_device(): pl.pallas_call(functools.partial(kernel, n, tp, group, share, deep), name...  203 us
    unnamed x9, local copies, waits for them, and re-layouts  11.2 us

profile of v1, /device:TPU:0, one launch (start us, length us, event | category | flops | bytes accessed | tf_op | source)
XLA Modules:
  0.0 220.6 jit_solution(4992831498387222054)
XLA Ops:
  0.6 1.7 broadcast_in_dim.2.mix_ref
  2.4 0.7 add.8
  3.1 0.6 reshape.22.norm_ref
  3.6 202.7 %mix_and_spread.1 = (bf16[288,9216]{1,0:T(8,128)(2,1)}, bf16[288,9216]{1,0:T(8,128)(2,1)}, bf16[288,9216]{1,0:T(8,128)(2,1)}, f32[6,1,1152]{2,1,0:T(1,128)}, f32[32,1,384]{2,1,0:T(1,128)}) custom-call(f32[1152,128]{1,0:T(8,128)} %broadcast_in_dim.2.mix_ref, f32[1,1,384]{2,1,0:T(1,128)} %reshape.22.norm_ref, f32[1152,2304]{1,0:T(8,128)} %fq.1, ...), custom_call_target="tpu_custom_call" | custom-call | tf_op jit(solution)/shard_map/mix_and_spread/pallas_call | solution.py:236
  206.3 0.8 reduce
  207.1 0.7 dynamic-slice_reduce_fusion
  207.8 0.9 fusion
  208.8 0.0 slice-start
  208.8 0.7 convert_element_type.6
  209.5 0.0 copy-start
  209.5 0.0 slice-start.1
  209.5 5.7 %copy.19 = bf16[9216,288]{0,1:T(8,128)(2,1)} copy(bf16[9216,288]{0,1:T(8,128)(2,1)} %bitcast.7) | data formatting | bytes 10616832
  215.2 0.0 copy-done
  215.2 2.5 %copy.20 = bf16[9216,288]{0,1:T(8,128)(2,1)} copy(bf16[9216,288]{0,1:T(8,128)(2,1)S(1)} %bitcast.6) | data formatting | bytes 10616832
  217.7 0.0 slice-done
  217.7 0.6 slice-done.1
  218.3 2.4 %copy.21 = bf16[9216,288]{0,1:T(8,128)(2,1)} copy(bf16[9216,288]{0,1:T(8,128)(2,1)S(1)} %bitcast.5) | data formatting | bytes 10616832
  (3 shorter events, 0.0 us)
Async XLA Ops:
  208.8 8.9 %slice-start = ((s8[5308416]{0:T(1024)(128)(4,1)}), s8[1114112]{0:T(1024)(128)(4,1)S(1)}, s32[]{:S(2)}) async-start(s8[5308416]{0:T(1024)(128)(4,1)} %bitcast.3), calls=%async_computation | async-start | bytes 2228224
  209.5 5.7 %copy-start = (bf16[288,9216]{1,0:T(8,128)(2,1)S(1)}, bf16[288,9216]{1,0:T(8,128)(2,1)}, u32[]{:S(2)}) copy-start(bf16[288,9216]{1,0:T(8,128)(2,1)} %get-tuple-element.13) | copy-start | bytes 15925252
  209.5 8.8 %slice-start.1 = ((s8[5308416]{0:T(1024)(128)(4,1)}), s8[4194304]{0:T(1024)(128)(4,1)S(1)}, s32[]{:S(2)}) async-start(s8[5308416]{0:T(1024)(128)(4,1)} %bitcast.3), calls=%async_computation.1 | async-start | bytes 8388608
